TPU v7x, 256 devices: a whole 4x4x8 slice. The times are simulated.
256 devices in a mesh: ctx: 64 (over z, x_hi, y), tp: 4 (over x_lo, core).
Axes of the slice: x: 4 (x_hi: 2, x_lo: 2; x = x_hi * 2 + x_lo), y: 4, z: 8, core: 2. Of those that a mesh axis runs over, the one named last changes fastest.
Arguments:
- queries: bfloat16 [9216, 3072], P('ctx', 'tp'), may hold values from -8 to 8
- keys: bfloat16 [9216, 3072], P('ctx', 'tp'), may hold values from -8 to 8
- values: bfloat16 [9216, 3072], P('ctx', 'tp'), may hold values from -6 to 6
- positions: int32 [9216], P('ctx'), may hold values from 0 to 9215, as said below
- lambda_vecs: float32 [4, 12, 128], P(None, 'tp'), may hold values from -0.6 to 0.6
- head_gain: float32 [3072], P('tp'), may hold values from 0.5 to 1.5
- out_weight: bfloat16 [3072, 5120], P('tp'), may hold values from -0.109375 to 0.109375
- residual: bfloat16 [9216, 5120], P('ctx', 'tp'), may hold values from -3 to 3
Outputs:
- mixed: bfloat16 [9216, 5120], P('ctx', 'tp')
Inputs may be any that keep to these rules, and one draw needn't show every extreme that they name: Each aligned run of 72 rows holds 72 consecutive positions in increasing order; the runs' first positions are the multiples of 72, each once.
All inputs are finite; a program needn't handle non-finite values.
Results may differ from a plain program's by a relative error of at most 0.012.
Values may be sent and summed in bfloat16 or wider, within the bound.
No kernel may reach another device: no remote copies, remote signals or barrier semaphores. Data moves between devices by JAX's collectives and lax.ppermute only.
A program may use at most 192 MiB of HBM per device.

v0:
```python
import math
import jax
import jax.numpy as jnp
from jax import lax
from jax.sharding import PartitionSpec as P

lambda_init = 0.2
out_factor = 0.8
norm_eps = 1e-05


def per_device(queries, keys, values, positions, lambda_vecs, head_gain, out_weight, residual):
    row_count = queries.shape[0]
    head_count = lambda_vecs.shape[1]
    head_depth = lambda_vecs.shape[2]
    score_scale = 1.0 / math.sqrt(head_depth)
    query_heads = queries.reshape(row_count, head_count, 2, head_depth)
    all_positions = lax.all_gather(positions, "ctx", axis=0, tiled=True)
    key_piece = lax.all_gather(keys, "ctx", axis=0, tiled=True)
    value_piece = lax.all_gather(values, "ctx", axis=0, tiled=True)
    piece_rows = key_piece.shape[0]
    allowed = all_positions[None, :] <= positions[:, None]
    highest = jnp.full((2, head_count, row_count), -1e30, jnp.float32)
    scores = (
        jnp.einsum(
            "ihad,jhad->ahij",
            query_heads,
            key_piece.reshape(piece_rows, head_count, 2, head_depth),
            preferred_element_type=jnp.float32,
        )
        * score_scale
    )
    scores = jnp.where(allowed, scores, -jnp.inf)
    fresh = jnp.maximum(highest, jnp.max(scores, -1))
    expo = jnp.where(allowed, jnp.exp(scores - fresh[..., None]), 0.0)
    total = jnp.sum(expo, -1)
    numerator = jnp.einsum(
        "ahij,jhe->ahie",
        expo.astype(jnp.bfloat16),
        value_piece.reshape(piece_rows, head_count, 2 * head_depth),
        preferred_element_type=jnp.float32,
    )
    highest, total, numerator = (fresh, total, numerator)
    attn = numerator / total[..., None]
    lambda_head = (
        jnp.exp(jnp.sum(lambda_vecs[0] * lambda_vecs[1], -1))
        - jnp.exp(jnp.sum(lambda_vecs[2] * lambda_vecs[3], -1))
        + lambda_init
    )
    diff = attn[0] - lambda_head[:, None, None] * attn[1]
    mean_square = jnp.mean(diff * diff, -1, keepdims=True)
    normed = (
        out_factor
        * diff
        / jnp.sqrt(mean_square + norm_eps)
        * head_gain.reshape(head_count, 1, 2 * head_depth)
    )
    normed = (
        jnp.transpose(normed, (1, 0, 2))
        .reshape(row_count, head_count * 2 * head_depth)
        .astype(jnp.bfloat16)
    )
    shares = lax.psum_scatter(
        lax.dot_general(
            out_weight, normed, (((0,), (1,)), ((), ())), preferred_element_type=jnp.float32
        ).astype(jnp.bfloat16),
        "tp",
        scatter_dimension=0,
        tiled=True,
    ).astype(jnp.float32)
    projected = jnp.transpose(shares)
    return (projected + residual.astype(jnp.float32)).astype(jnp.bfloat16)


def solution(mesh):
    placed = (
        P("ctx", "tp"),
        P("ctx", "tp"),
        P("ctx", "tp"),
        P("ctx"),
        P(None, "tp", None),
        P("tp"),
        P("tp", None),
        P("ctx", "tp"),
    )
    return jax.shard_map(
        per_device, mesh=mesh, in_specs=placed, out_specs=P("ctx", "tp"), check_vma=False
    )
```

profile of v0, /device:TPU:1, one launch (start us, length us, event | category | flops | bytes accessed | tf_op | source)
XLA Modules:
  0.0 507.1 jit_solution(6777662970282332329)
XLA Ops:
  6.5 0.0 all-gather.3.cloned.1.call-start
  6.5 0.7 all-gather.3.cloned.1.call-update
  7.3 0.0 all-gather.5.cloned.1.call-start
  7.3 0.7 all-gather.5.cloned.1.call-update
  8.0 0.0 reduce-scatter.2.cloned.1.call-start
  8.1 1.0 reshape.37
  9.1 0.7 mul.50
  9.8 1.3 dynamic-slice
  11.7 0.9 dynamic-update-slice
  12.6 310.0 %all-reduce = s32[9216]{0:T(1024)S(1)} all-reduce(s32[9216]{0:T(1024)S(1)} %dynamic-update-slice), channel_id=1, replica_groups=mesh['ctx'=64,'tp'=4] {'ctx'}, use_global_device_ids=true, to_apply=%add | all-reduce | flops 9216 | bytes 73728
  322.6 0.9 multiply_reduce_fusion.2
  323.6 1.4 broadcast_compare_fusion
  325.0 0.0 all-gather.3.cloned.1.call-done
  325.0 18.7 %copy.20 = bf16[9216,768]{0,1:T(8,128)(2,1)} copy(bf16[9216,768]{1,0:T(8,128)(2,1)} %all-gather.3.cloned.1.call-done) | data formatting | bytes 28311552 | tf_op jit(solution)/shard_map/all_gather | solution.py:19
  343.7 16.2 %fusion = (f32[2,3,144]{2,1,0:T(4,128)S(1)}, f32[2,3,144,9216]{3,2,1,0:T(8,128)}) fusion(pred[144,9216]{1,0:T(8,128)(4,1)S(1)} %broadcast_compare_fusion, bf16[9216,3,2,128]{0,3,2,1:T(8,128)(2,1)} %bitcast.44, bf16[144,3,2,128]{3,2,1,0:T(2,128)(2,1)S(1)} %reshape.37), kind=kOutput, calls=%fused_computation.2 | convolution fusion | flops 2062318720 | bytes 47558016 | tf_op jit(solution)/shard_map/ihad,jhad->ahij/dot_general | solution.py:25
  359.9 20.7 %fusion.1 = (f32[2,3,144]{2,1,0:T(4,128)S(1)}, bf16[2,3,144,9216]{3,2,1,0:T(8,128)(2,1)}) fusion(f32[2,3,144,9216]{3,2,1,0:T(8,128)} %get-tuple-element.10, f32[2,3,144]{2,1,0:T(4,128)S(1)} %broadcast_maximum_fusion, pred[144,9216]{1,0:T(8,128)(4,1)S(1)} %broadcast_compare_fusion), kind=kLoop, calls=%fused_computation.3 | loop fusion | flops 47774880 | bytes 49109760 | tf_op jit(solution)/shard_map/reduce_sum | solution.py:36
  380.6 16.6 %all-gather.5.cloned.1.call-done = bf16[9216,768]{1,0:T(8,128)(2,1)} async-done(((bf16[144,768]{1,0:T(8,128)(2,1)}), bf16[9216,768]{1,0:T(8,128)(2,1)}) %all-gather.5.cloned.1.call-update) | async-done | bytes 14155792 | tf_op jit(solution)/shard_map/all_gather | solution.py:20
  397.2 17.8 %copy.23 = bf16[9216,768]{0,1:T(8,128)(2,1)} copy(bf16[9216,768]{1,0:T(8,128)(2,1)} %all-gather.5.cloned.1.call-done) | data formatting | bytes 28311552 | tf_op jit(solution)/shard_map/all_gather | solution.py:20
  415.0 20.3 %fusion.11 = f32[2,3,144,256]{3,2,0,1:T(8,128)S(1)} fusion(bf16[9216,3,256,1]{0,2,3,1:T(8,128)(2,1)} %bitcast.45, bf16[2,3,144,9216]{3,2,1,0:T(8,128)(2,1)} %get-tuple-element.8, f32[2,3,144]{2,0,1:T(2,128)S(1)} %copy.26), kind=kOutput, calls=%fused_computation.13 | convolution fusion | flops 4077084672 | bytes 30969216 | tf_op jit(solution)/shard_map/ahij,jhe->ahie/dot_general | solution.py:37
  435.2 0.0 copy-start
  435.3 0.3 multiply_reduce_fusion
  435.5 0.2 fusion.18
  435.7 5.7 %fusion.7 = bf16[5120,144]{0,1:T(8,128)(2,1)} fusion(bf16[144,768]{1,0:T(8,128)(2,1)S(1)} %bitcast.46, bf16[768,5120]{1,0:T(8,128)(2,1)} %param.14), kind=kOutput, calls=%fused_computation.10 | convolution fusion | flops 1133199360 | bytes 9560064 | tf_op jit(solution)/shard_map/dot_general | solution.py:64
  441.5 0.0 reduce-scatter.2.cloned.1.call-update
  441.5 57.3 %reduce-scatter.2.cloned.1.call-done = bf16[1280,144]{0,1:T(8,128)(2,1)} async-done(((bf16[5120,144]{0,1:T(8,128)(2,1)}), bf16[1280,144]{0,1:T(8,128)(2,1)}) %reduce-scatter.2.cloned.1.call-update) | async-done | bytes 368656 | tf_op jit(solution)/shard_map/reduce_scatter | solution.py:63
  498.8 0.0 copy-done
  498.8 1.8 fusion.14
  (6 shorter events, 0.1 us)
Async XLA Ops:
  6.5 318.5 %all-gather.3.cloned.1.call-start = ((), (), s32[]{:S(2)}) async-start(), calls=%async_computation.1 | async-start | bytes 14376960 | tf_op jit(solution)/shard_map/all_gather | solution.py:19
  7.3 390.0 %all-gather.5.cloned.1.call-start = ((), (), s32[]{:S(2)}) async-start(), calls=%async_computation.2 | async-start | bytes 14376960 | tf_op jit(solution)/shard_map/all_gather | solution.py:20
  8.0 490.8 %reduce-scatter.2.cloned.1.call-start = ((), (), s32[]{:S(2)}) async-start(), calls=%async_computation.3 | async-start | bytes 1843200 | tf_op jit(solution)/shard_map/reduce_scatter | solution.py:63
  435.2 63.5 %copy-start = (bf16[144,1280]{1,0:T(8,128)(2,1)S(1)}, bf16[144,1280]{1,0:T(8,128)(2,1)}, u32[]{:S(2)}) copy-start(bf16[144,1280]{1,0:T(8,128)(2,1)} %param.15) | copy-start | bytes 1105924
Sparse Core Ops, SparseCore 0:
  11.0 194.6 all-gather.2
  209.4 187.7 all-gather.4
  441.6 57.1 reduce-scatter.1
where the time goes:
time: 508 us; the launch traced here: 507 us
  blocking collectives  310 us (61%)
  waiting for transfers between devices  75.3 us (15%)
  matrix products  42.2 us (8%)
  local copies, waits for them, and re-layouts  40.3 us (8%)
  other arithmetic  25.4 us (5%)
  between operations  13.8 us (3%)
    unnamed x1, blocking collectives  310 us
    reduce_scatter x1, waiting for transfers between devices, per_device(): lax.psum_scatter(lax.dot_general(out_weight, normed, (((0,), (1,)), ((),...  57.3 us
    reduce_sum x1, other arithmetic, per_device(): total = jnp.sum(expo, -1)  20.7 us
    dot_general x1, matrix products, per_device(): jnp.einsum('ahij,jhe->ahie', expo.astype(jnp.bfloat16), value_piece.resha...  20.3 us
    all_gather x1, local copies, waits for them, and re-layouts, per_device(): key_piece = lax.all_gather(keys, 'ctx', axis=0, tiled=True)  18.7 us
    all_gather x1, local copies, waits for them, and re-layouts, per_device(): value_piece = lax.all_gather(values, 'ctx', axis=0, tiled=True)  17.8 us
    all_gather x1, waiting for transfers between devices, per_device(): value_piece = lax.all_gather(values, 'ctx', axis=0, tiled=True)  16.6 us
    dot_general x1, matrix products, per_device(): jnp.einsum('ihad,jhad->ahij', query_heads, key_piece.reshape(piece_rows,...  16.2 us
  transfers between devices with their start and end apart: 3, of which 2 were waited for; matrix products, arithmetic and copies ran while one was open for 12% of the time, Pallas kernels for 0%

commit v1 on v0

--- a/solution.py
+++ b/solution.py
@@ -1,3 +1,4 @@
+import functools
 import math
 import jax
 import jax.numpy as jnp
@@ -9,6 +10,16 @@
 norm_eps = 1e-05
 
 
+def raise_terms_by_axis(sheet, shard_axis, axis_k):
+    low = jnp.stack(lax.psum(1, axis_name=shard_axis) * [sheet])
+    return jnp.concatenate(
+        lax.all_to_all(low, axis_name=shard_axis, split_axis=0, concat_axis=0), axis=axis_k
+    )
+
+
+_drive_quotas = functools.partial(raise_terms_by_axis, shard_axis="ctx", axis_k=0)
+
+
 def per_device(queries, keys, values, positions, lambda_vecs, head_gain, out_weight, residual):
     row_count = queries.shape[0]
     head_count = lambda_vecs.shape[1]
@@ -16,7 +27,7 @@
     score_scale = 1.0 / math.sqrt(head_depth)
     query_heads = queries.reshape(row_count, head_count, 2, head_depth)
     all_positions = lax.all_gather(positions, "ctx", axis=0, tiled=True)
-    key_piece = lax.all_gather(keys, "ctx", axis=0, tiled=True)
+    key_piece = _drive_quotas(keys)
     value_piece = lax.all_gather(values, "ctx", axis=0, tiled=True)
     piece_rows = key_piece.shape[0]
     allowed = all_positions[None, :] <= positions[:, None]

time: 508 us -> 873 us (1.72)
  blocking collectives: 310 us -> 645 us
  starting transfers between devices: 0.08 us -> 15.6 us
  local copies, waits for them, and re-layouts: 40.3 us -> 52.8 us
    unnamed x1, blocking collectives: 310 us -> 645 us
    another operation x0 -> x2, local copies, waits for them, and re-layouts: none -> 34 us  [the longest x1 27 us: per_device(): key_piece.reshape(piece_rows, head_count, 2, head_depth)]
    all_gather x1 -> x0, local copies, waits for them, and re-layouts: 18.7 us -> none  [per_device(): key_piece = lax.all_gather(keys, 'ctx', axis=0, tiled=True)]
    reduce_scatter x1, waiting for transfers between devices: 57.3 us -> 74.4 us  [per_device(): lax.psum_scatter(lax.dot_general(out_weight, normed, (((0,), (1,)), ((),...]
    all_gather x1, waiting for transfers between devices: 16.6 us -> 0.01 us  [per_device(): value_piece = lax.all_gather(values, 'ctx', axis=0, tiled=True)]
    all_to_all x0 -> x1, starting transfers between devices: none -> 15.5 us  [raise_terms_by_axis(): lax.all_to_all(low, axis_name=shard_axis, split_axis=0, concat_axis=0)]
  transfers between devices with their start and end apart: 3 -> 3, of which waited for: 2 -> 1; matrix products, arithmetic and copies ran while one was open for 12% -> 8% of each run, Pallas kernels for 0% -> 0%
where the time goes in v1:
time: 873 us; the launch traced here: 872 us
  blocking collectives  645 us (74%)
  waiting for transfers between devices  75.2 us (9%)
  local copies, waits for them, and re-layouts  52.8 us (6%)
  matrix products  45 us (5%)
  other arithmetic  23.7 us (3%)
  starting transfers between devices  15.6 us (2%)
  between operations  14.2 us (2%)
    unnamed x1, blocking collectives  645 us
    reduce_scatter x1, waiting for transfers between devices, per_device(): lax.psum_scatter(lax.dot_general(out_weight, normed, (((0,), (1,)), ((),...  74.4 us
    another operation x1, local copies, waits for them, and re-layouts, per_device(): key_piece.reshape(piece_rows, head_count, 2, head_depth)  27 us
    reduce_sum x1, other arithmetic, per_device(): total = jnp.sum(expo, -1)  20.5 us
    dot_general x1, matrix products, per_device(): jnp.einsum('ahij,jhe->ahie', expo.astype(jnp.bfloat16), value_piece.resha...  20.3 us
    dot_general x1, matrix products, per_device(): jnp.einsum('ihad,jhad->ahij', query_heads, key_piece.reshape(piece_rows,...  19 us
    all_gather x1, local copies, waits for them, and re-layouts, per_device(): value_piece = lax.all_gather(values, 'ctx', axis=0, tiled=True)  17.8 us
  transfers between devices with their start and end apart: 3, of which 1 were waited for; matrix products, arithmetic and copies ran while one was open for 8% of the time, Pallas kernels for 0%

profile of v1, /device:TPU:1, one launch (start us, length us, event | category | flops | bytes accessed | tf_op | source)
XLA Modules:
  0.0 871.5 jit_solution(13847423320329387765)
XLA Ops:
  6.5 7.0 stack.2
  13.5 0.0 copy-start.1
  13.5 0.0 copy-start.4
  13.5 0.0 copy-start.5
  13.5 0.0 copy-start.3
  13.5 0.0 copy-start.2
  13.5 15.5 %all-to-all-start = ((bf16[64,144,768]{2,1,0:T(8,128)(2,1)}), bf16[64,144,768]{2,1,0:T(8,128)(2,1)}, u32[]{:S(2)}, u32[]{:S(2)}) async-start(bf16[64,144,768]{2,1,0:T(8,128)(2,1)} %stack.2), calls=%async_computation | async-start | bytes 28311552 | tf_op jit(solution)/shard_map/all_to_all | solution.py:16
  29.0 0.0 all-gather.2.cloned.1.call-start
  29.1 0.7 all-gather.2.cloned.1.call-update
  29.8 0.0 reduce-scatter.2.cloned.1.call-start
  29.8 0.0 copy-done.1
  29.8 0.1 reshape.36
  29.9 0.0 copy-done.4
  29.9 0.0 copy-done.5
  29.9 0.6 dynamic-slice
  31.2 0.0 copy-done.3
  31.2 0.3 dynamic-update-slice
  31.5 645.1 %all-reduce = s32[9216]{0:T(1024)S(1)} all-reduce(s32[9216]{0:T(1024)S(1)} %dynamic-update-slice), channel_id=1, replica_groups=mesh['ctx'=64,'tp'=4] {'ctx'}, use_global_device_ids=true, to_apply=%add | all-reduce | flops 9216 | bytes 73728
  676.6 0.0 copy-done.2
  676.6 0.1 multiply_reduce_fusion.2
  676.7 0.8 broadcast_compare_fusion
  677.5 0.0 all-to-all-done
  677.5 27.0 %reshape_reshape.3 = bf16[9216,3,2,128]{3,2,1,0:T(2,128)(2,1)} reshape(bf16[64,144,768]{2,1,0:T(8,128)(2,1)} %all-to-all-done) | data formatting | bytes 28311552 | tf_op jit(solution)/shard_map/reshape;reshape | solution.py:39
  704.5 19.0 %fusion = (f32[2,3,144]{2,1,0:T(4,128)S(1)}, f32[2,3,144,9216]{3,2,1,0:T(8,128)}) fusion(pred[144,9216]{1,0:T(8,128)(4,1)S(1)} %broadcast_compare_fusion, bf16[9216,3,2,128]{3,2,1,0:T(2,128)(2,1)} %reshape_reshape.3, bf16[144,3,2,128]{3,2,1,0:T(2,128)(2,1)S(1)} %reshape.36), kind=kOutput, calls=%fused_computation.2 | convolution fusion | flops 2062318720 | bytes 47558016 | tf_op jit(solution)/shard_map/ihad,jhad->ahij/dot_general | solution.py:36
  723.6 20.5 %fusion.1 = (f32[2,3,144]{2,1,0:T(4,128)S(1)}, bf16[2,3,144,9216]{3,2,1,0:T(8,128)(2,1)}) fusion(f32[2,3,144,9216]{3,2,1,0:T(8,128)} %get-tuple-element.10, f32[2,3,144]{2,1,0:T(4,128)S(1)} %broadcast_maximum_fusion, pred[144,9216]{1,0:T(8,128)(4,1)S(1)} %broadcast_compare_fusion), kind=kLoop, calls=%fused_computation.3 | loop fusion | flops 47774880 | bytes 49109760 | tf_op jit(solution)/shard_map/reduce_sum | solution.py:47
  744.1 0.0 all-gather.2.cloned.1.call-done
  744.1 17.8 %copy.21 = bf16[9216,768]{0,1:T(8,128)(2,1)} copy(bf16[9216,768]{1,0:T(8,128)(2,1)} %all-gather.2.cloned.1.call-done) | data formatting | bytes 28311552 | tf_op jit(solution)/shard_map/all_gather | solution.py:31
  761.9 20.3 %fusion.11 = f32[2,3,144,256]{3,2,0,1:T(8,128)S(1)} fusion(bf16[9216,3,256,1]{0,2,3,1:T(8,128)(2,1)} %bitcast.43, bf16[2,3,144,9216]{3,2,1,0:T(8,128)(2,1)} %get-tuple-element.8, f32[2,3,144]{2,0,1:T(2,128)S(1)} %copy.24), kind=kOutput, calls=%fused_computation.13 | convolution fusion | flops 4077084672 | bytes 30969216 | tf_op jit(solution)/shard_map/ahij,jhe->ahie/dot_general | solution.py:48
  782.2 0.0 copy-start
  782.2 0.3 multiply_reduce_fusion
  782.4 0.2 fusion.18
  782.6 5.7 fusion.7
  788.4 0.0 reduce-scatter.2.cloned.1.call-update
  788.4 74.4 %reduce-scatter.2.cloned.1.call-done = bf16[1280,144]{0,1:T(8,128)(2,1)} async-done(((bf16[5120,144]{0,1:T(8,128)(2,1)}), bf16[1280,144]{0,1:T(8,128)(2,1)}) %reduce-scatter.2.cloned.1.call-update) | async-done | bytes 368656 | tf_op jit(solution)/shard_map/reduce_scatter | solution.py:74
  862.8 0.0 copy-done
  862.9 1.8 fusion.14
  (7 shorter events, 0.1 us)
Async XLA Ops:
  13.5 16.3 %copy-start.1 = (bf16[144,768]{1,0:T(8,128)(2,1)S(1)}, bf16[144,768]{1,0:T(8,128)(2,1)}, u32[]{:S(2)}) copy-start(bf16[144,768]{1,0:T(8,128)(2,1)} %param.8) | copy-start | bytes 663556
  13.5 16.4 %copy-start.4 = (f32[768]{0:T(1024)S(1)}, f32[768]{0:T(1024)}, u32[]{:S(2)}) copy-start(f32[768]{0:T(1024)} %param.13) | copy-start | bytes 9220
  13.5 16.4 %copy-start.5 = (u32[256]{0:T(256)S(1)}, u32[256]{0:T(256)}, u32[]{:S(2)}) copy-start(u32[256]{0:T(256)} %constant.25) | copy-start | bytes 3076
  13.5 17.7 %copy-start.3 = (s32[144]{0:T(256)S(1)}, s32[144]{0:T(256)}, u32[]{:S(2)}) copy-start(s32[144]{0:T(256)} %param.11) | copy-start | bytes 1732
  13.5 663.1 %copy-start.2 = (f32[4,3,128]{2,0,1:T(4,128)S(1)}, f32[4,3,128]{2,0,1:T(4,128)}, u32[]{:S(2)}) copy-start(f32[4,3,128]{2,0,1:T(4,128)} %param.12) | copy-start | bytes 18436
  13.5 664.0 %all-to-all-start = ((bf16[64,144,768]{2,1,0:T(8,128)(2,1)}), bf16[64,144,768]{2,1,0:T(8,128)(2,1)}, u32[]{:S(2)}, u32[]{:S(2)}) async-start(bf16[64,144,768]{2,1,0:T(8,128)(2,1)} %stack.2), calls=%async_computation | async-start | bytes 28311552 | tf_op jit(solution)/shard_map/all_to_all | solution.py:16
  29.0 715.1 %all-gather.2.cloned.1.call-start = ((), (), s32[]{:S(2)}) async-start(), calls=%async_computation.2 | async-start | bytes 14376960 | tf_op jit(solution)/shard_map/all_gather | solution.py:31
  29.8 833.1 %reduce-scatter.2.cloned.1.call-start = ((), (), s32[]{:S(2)}) async-start(), calls=%async_computation.3 | async-start | bytes 1843200 | tf_op jit(solution)/shard_map/reduce_scatter | solution.py:74
  782.2 80.7 %copy-start = (bf16[144,1280]{1,0:T(8,128)(2,1)S(1)}, bf16[144,1280]{1,0:T(8,128)(2,1)}, u32[]{:S(2)}) copy-start(bf16[144,1280]{1,0:T(8,128)(2,1)} %param.15) | copy-start | bytes 1105924
Sparse Core Ops, SparseCore 0:
  33.5 379.2 all-gather.1
  788.5 74.2 reduce-scatter.1
